TPU v7x, 32 devices: a whole 2x2x4 slice. The times are simulated.
32 devices in a mesh: groups: 2 (over x), tile: 16 (over z, y, core).
Axes of the slice: x: 2, y: 2, z: 4, core: 2. Of those that a mesh axis runs over, the one named last changes fastest.
Arguments:
- probes: float32 [8, 262144], P(None, ('groups', 'tile')), parts along dimension 1, may hold values from -6 to 6
- level_set: float32 [262144], P(('groups', 'tile')), parts along dimension 0, may hold values from -6 to 6
- unit_label: int32 [262144], P(('groups', 'tile')), parts along dimension 0, may hold values from 0 to 3
- contrast: float32 [8], P('groups'), parts along dimension 0, may hold values from 0.2 to 1.5
- station_weight: float32 [65536], P('groups'), parts along dimension 0, may hold values from 0.2 to 2
- u_factor: bfloat16 [4096, 32, 512], P(('groups', 'tile')), parts along dimension 0, may hold values from -1 to 1
- v_factor: bfloat16 [4096, 32, 512], P(('groups', 'tile')), parts along dimension 0, may hold values from -0.25 to 0.25
- col_owner: int32 [4096, 1], P('groups'), parts along dimension 0, may hold values from 0 to 15; in each aligned block of 128 rows (0 to 127, 128 to 255, ...) at most 16 rows name the same one
- col_local: int32 [4096], P('groups'), parts along dimension 0, may hold values from 0 to 15
- row_owner: int32 [4096, 1], P('groups'), parts along dimension 0, may hold values from 0 to 15; in each aligned block of 128 rows (0 to 127, 128 to 255, ...) at most 16 rows name the same one
- row_local: int32 [4096], P('groups'), parts along dimension 0, may hold values from 0 to 3
- tile_rank: int32 [4096], P('groups'), parts along dimension 0, may hold values from 8 to 32
Outputs:
- hessian_probes: float32 [8, 262144], P(None, ('groups', 'tile')), parts along dimension 1
There are 2 independent parts, one for each index of `groups`. A program takes and returns all parts, laid end to end along the dimension named above; each array names one. Nothing has to cross between parts.
Inputs may be any that keep to these rules, and one draw needn't show every extreme that they name: `col_owner`: among the 128 tiles of one device (aligned blocks of 128 entries) no owner is named more than 16 times, a bound that some block reaches. `row_owner`: among the 128 tiles of one device (aligned blocks of 128 entries) no owner is named more than 16 times, a bound that some block reaches.
All inputs are finite; a program needn't handle non-finite values.
Results may differ from a plain program's by a relative error of at most 0.005.
Values may be sent and summed in bfloat16 or wider, within the bound.
No kernel may reach another device: no remote copies, remote signals or barrier semaphores. Data moves between devices by JAX's collectives and lax.ppermute only.
A program may use at most 64 MiB of HBM per device.

v0:
```python
import jax
import jax.numpy as jnp
from jax import lax
from jax.sharding import PartitionSpec as P

HIGHEST = lax.Precision.HIGHEST


def rank_within(owner_table, target, capacity):
    matches = (owner_table == target).astype(jnp.int32)
    position = jnp.cumsum(matches, axis=-1) - 1
    slot_ids = jnp.arange(capacity, dtype=jnp.int32)
    chosen = (matches[:, None, :] == 1) & (position[:, None, :] == slot_ids[None, :, None])
    return chosen.astype(jnp.float32)


def sender_table(owner_table, local_table, target, capacity, block_count):
    chosen = rank_within(owner_table, target, capacity)
    local_match = (
        local_table[:, :, None] == jnp.arange(block_count, dtype=jnp.int32)[None, None, :]
    ).astype(jnp.float32)
    return jnp.einsum(
        "pqs,psb->pqb", chosen, local_match, precision=HIGHEST, preferred_element_type=jnp.float32
    )


def receiver_table(owner_mine, capacity, peer_count):
    count = owner_mine.shape[0]
    positions = jnp.arange(count, dtype=jnp.int32)
    earlier = (owner_mine[None, :] == owner_mine[:, None]) & (
        positions[None, :] < positions[:, None]
    )
    order = jnp.sum(earlier.astype(jnp.int32), axis=1)
    target = owner_mine * capacity + order
    return (target[:, None] == jnp.arange(peer_count * capacity, dtype=jnp.int32)[None, :]).astype(
        jnp.float32
    )


def shards(
    probes,
    level_set,
    unit_label,
    contrast,
    station_weight,
    u_factor,
    v_factor,
    col_owner,
    col_local,
    row_owner,
    row_local,
    tile_rank,
):
    peer_count = lax.axis_size("tile")
    own_index = lax.axis_index("tile")
    tile_count, rank_max, station_width = u_factor.shape
    cell_width = v_factor.shape[2]
    probe_count, cell_total = probes.shape
    cell_blocks = cell_total // cell_width
    station_blocks = station_weight.shape[0] // (peer_count * station_width)
    capacity = max(2, 2 * tile_count // peer_count)
    flat_cells = probe_count * cell_width
    flat_stations = probe_count * station_width
    col_owner_all = col_owner.reshape(peer_count, tile_count)
    col_local_all = col_local.reshape(peer_count, tile_count)
    row_owner_all = row_owner.reshape(peer_count, tile_count)
    row_local_all = row_local.reshape(peer_count, tile_count)
    col_owner_mine = lax.dynamic_index_in_dim(col_owner_all, own_index, 0, keepdims=False)
    col_local_mine = lax.dynamic_index_in_dim(col_local_all, own_index, 0, keepdims=False)
    row_owner_mine = lax.dynamic_index_in_dim(row_owner_all, own_index, 0, keepdims=False)
    row_local_mine = lax.dynamic_index_in_dim(row_local_all, own_index, 0, keepdims=False)
    rank_mine = lax.dynamic_index_in_dim(
        tile_rank.reshape(peer_count, tile_count), own_index, 0, keepdims=False
    )
    unit_count = contrast.shape[0]
    unit_match = (unit_label[None, :] == jnp.arange(unit_count, dtype=jnp.int32)[:, None]).astype(
        jnp.float32
    )
    scaling = jnp.sum(unit_match * contrast[:, None], axis=0) / (1.0 + level_set * level_set)
    scaled = (probes * scaling[None, :]).astype(jnp.bfloat16)
    cell_rows = (
        scaled.reshape(probe_count, cell_blocks, cell_width)
        .transpose(1, 0, 2)
        .reshape(cell_blocks, flat_cells)
    )
    col_global = col_owner_mine * cell_blocks + col_local_mine
    col_slots = receiver_table(col_owner_mine, capacity, peer_count)
    col_choice = sender_table(col_owner_all, col_local_all, own_index, capacity, cell_blocks)
    piece = lax.all_gather(cell_rows, "tile", axis=0, tiled=True)
    rows_here = piece.shape[0]
    match = (col_global[:, None] == jnp.arange(rows_here, dtype=jnp.int32)[None, :]).astype(
        jnp.bfloat16
    )
    fetched = jnp.dot(match, piece, preferred_element_type=jnp.float32)
    tile_cells = fetched.astype(jnp.bfloat16).reshape(tile_count, probe_count, cell_width)
    keep = (jnp.arange(rank_max, dtype=jnp.int32)[None, :] < rank_mine[:, None]).astype(
        jnp.float32
    )[:, None, :]
    coeff = jnp.einsum("tkc,trc->tkr", tile_cells, v_factor, preferred_element_type=jnp.float32)
    coeff = (coeff * keep).astype(jnp.bfloat16)
    partial_value = jnp.einsum(
        "tkr,trs->tks", coeff, u_factor, preferred_element_type=jnp.float32
    ).reshape(tile_count, flat_stations)
    row_global = row_owner_mine * station_blocks + row_local_mine
    match = (
        jnp.arange(station_blocks * lax.axis_size("tile"), dtype=jnp.int32)[:, None]
        == row_global[None, :]
    ).astype(jnp.float32)
    predicted = lax.psum_scatter(
        jnp.dot(match, partial_value, precision=HIGHEST, preferred_element_type=jnp.float32),
        "tile",
        scatter_dimension=0,
        tiled=True,
    )
    weight_mine = lax.dynamic_slice_in_dim(
        station_weight, own_index * station_blocks * station_width, station_blocks * station_width
    )
    weighted = (
        predicted.reshape(station_blocks, probe_count, station_width)
        * weight_mine.reshape(station_blocks, 1, station_width)
    ).astype(jnp.bfloat16)
    weighted = weighted.reshape(station_blocks, flat_stations)
    row_choice = sender_table(row_owner_all, row_local_all, own_index, capacity, station_blocks)
    outgoing_data = jnp.einsum(
        "pqb,bf->pqf", row_choice.astype(jnp.bfloat16), weighted, preferred_element_type=jnp.float32
    ).astype(jnp.bfloat16)
    incoming_data = lax.all_to_all(outgoing_data, "tile", split_axis=0, concat_axis=0, tiled=True)
    row_slots = receiver_table(row_owner_mine, capacity, peer_count)
    tile_data = jnp.dot(
        row_slots.astype(jnp.bfloat16),
        incoming_data.reshape(peer_count * capacity, flat_stations),
        preferred_element_type=jnp.float32,
    )
    tile_weighted = tile_data.astype(jnp.bfloat16).reshape(tile_count, probe_count, station_width)
    back = jnp.einsum("tks,trs->tkr", tile_weighted, u_factor, preferred_element_type=jnp.float32)
    back = (back * keep).astype(jnp.bfloat16)
    spread = jnp.einsum("tkr,trc->tkc", back, v_factor, preferred_element_type=jnp.float32).reshape(
        tile_count, flat_cells
    )
    slot_rows = col_slots.T.reshape(peer_count, capacity, tile_count)
    returned = jnp.einsum(
        "pqt,tf->pqf", slot_rows, spread, precision=HIGHEST, preferred_element_type=jnp.float32
    )
    arrived = lax.all_to_all(returned, "tile", split_axis=0, concat_axis=0, tiled=True)
    summed = jnp.einsum(
        "pqb,pqf->bf", col_choice, arrived, precision=HIGHEST, preferred_element_type=jnp.float32
    )
    gradient = (
        summed.reshape(cell_blocks, probe_count, cell_width)
        .transpose(1, 0, 2)
        .reshape(probe_count, cell_total)
    )
    return scaling[None, :] * gradient


def solution(mesh):
    placed = (
        P(None, ("groups", "tile")),
        P(("groups", "tile")),
        P(("groups", "tile")),
        P("groups"),
        P("groups"),
        P(("groups", "tile"), None, None),
        P(("groups", "tile"), None, None),
        P("groups", None),
        P("groups"),
        P("groups", None),
        P("groups"),
        P("groups"),
    )
    return jax.shard_map(
        shards, mesh=mesh, in_specs=placed, out_specs=P(None, ("groups", "tile")), check_vma=False
    )
```

profile of v0, /device:TPU:13, one launch (start us, length us, event | category | flops | bytes accessed | tf_op | source)
XLA Modules:
  0.0 335.7 jit_solution(17233125049416313303)
XLA Ops:
  6.5 0.9 select_reduce_fusion
  7.5 0.8 add_divide_fusion
  8.2 1.0 multiply_convert_fusion
  9.2 0.7 copy.15
  10.0 0.7 dynamic_slice.24
  10.7 0.7 fusion.35
  11.4 0.7 fusion.38
  12.3 38.9 %all-gather.2.cloned.1.call-done = bf16[256,4096]{1,0:T(8,128)(2,1)} async-done(((bf16[16,4096]{1,0:T(8,128)(2,1)}), bf16[256,4096]{1,0:T(8,128)(2,1)}) %all-gather.2.cloned.1.call-update) | async-done | bytes 2097168 | tf_op jit(solution)/shard_map/all_gather | solution.py:89
  51.2 2.1 convolution_convert_fusion.2
  53.2 0.4 copy.16
  53.6 5.2 %fusion.3 = f32[128,8,512]{2,1,0:T(8,128)S(1)} fusion(bf16[128,32,512]{2,1,0:T(8,128)(2,1)} %param.17, bf16[128,8,512]{2,1,0:T(8,128)(2,1)S(1)} %bitcast.63, bf16[128,32,512]{2,1,0:T(8,128)(2,1)} %param.18, f32[128,32]{1,0:T(8,128)S(1)} %fusion.23), kind=kOutput, calls=%fused_computation.8 | convolution fusion | flops 67174400 | bytes 11550720 | tf_op jit(solution)/shard_map/tkr,trs->tks/dot_general | solution.py:101
  58.8 1.6 copy.17
  60.5 1.9 fusion.28
  62.5 0.3 reduce_window_sum.18
  62.8 0.6 dynamic-slice
  64.3 89.8 %all-reduce.3.cloned.1.call-done = f32[64,4096]{1,0:T(8,128)} async-done(((f32[64,4096]{1,0:T(8,128)}), f32[64,4096]{1,0:T(8,128)}) %all-reduce.3.cloned.1.call-update) | async-done | bytes 1048592
  154.0 3.1 convolution_convert_fusion
  157.1 6.8 %all-to-all-start = ((bf16[16,16,4096]{2,1,0:T(8,128)(2,1)}), bf16[16,16,4096]{2,1,0:T(8,128)(2,1)S(1)}, u32[]{:S(2)}, u32[]{:S(2)}) async-start(bf16[16,16,4096]{2,1,0:T(8,128)(2,1)} %convolution_convert_fusion), calls=%async_computation | async-start | bytes 4194304 | tf_op jit(solution)/shard_map/all_to_all | solution.py:127
  163.9 0.2 convert_reduce_fusion
  164.0 0.2 convert_reduce_fusion.1
  164.3 47.0 %all-to-all-done = bf16[16,16,4096]{2,1,0:T(8,128)(2,1)S(1)} async-done(((bf16[16,16,4096]{2,1,0:T(8,128)(2,1)}), bf16[16,16,4096]{2,1,0:T(8,128)(2,1)S(1)}, u32[]{:S(2)}, u32[]{:S(2)}) %all-to-all-start) | async-done | bytes 2097184 | tf_op jit(solution)/shard_map/all_to_all | solution.py:127
  211.3 0.5 convolution_convert_fusion.1
  211.8 0.4 copy.19
  212.2 6.5 %fusion.2 = f32[128,8,512]{2,1,0:T(8,128)} fusion(bf16[128,32,512]{2,1,0:T(8,128)(2,1)} %param.18, bf16[128,8,512]{2,1,0:T(8,128)(2,1)S(1)} %bitcast.62, bf16[128,32,512]{2,1,0:T(8,128)(2,1)} %param.17, f32[128,32]{1,0:T(8,128)S(1)} %fusion.23), kind=kOutput, calls=%fused_computation.7 | convolution fusion | flops 67174400 | bytes 11550720 | tf_op jit(solution)/shard_map/tkr,trc->tkc/dot_general | solution.py:137
  218.7 1.7 reshape.169
  220.5 3.8 %fusion.11 = f32[16,16,4096]{2,1,0:T(8,128)} fusion(f32[128,4096,1]{1,0,2:T(8,128)S(1)} %reshape.169, s32[16,16]{1,0:T(8,128)S(1)} %multiply_add_fusion, s32[128]{0:T(128)S(1)} %multiply_add_fusion.2), kind=kOutput, calls=%fused_computation.25 | convolution fusion | flops 1610645504 | bytes 6292992 | tf_op jit(solution)/shard_map/pqt,tf->pqf/dot_general | solution.py:141
  224.3 5.0 %all-to-all-start.1 = ((f32[16,16,4096]{2,1,0:T(8,128)}), f32[16,16,4096]{2,1,0:T(8,128)}, u32[]{:S(2)}, u32[]{:S(2)}) async-start(f32[16,16,4096]{2,1,0:T(8,128)} %fusion.11), calls=%async_computation.1 | async-start | bytes 8388608 | tf_op jit(solution)/shard_map/all_to_all | solution.py:144
  229.4 0.3 reduce_window_sum.17
  229.7 0.2 fusion.7
  229.8 92.0 %all-to-all-done.1 = f32[16,16,4096]{2,1,0:T(8,128)} async-done(((f32[16,16,4096]{2,1,0:T(8,128)}), f32[16,16,4096]{2,1,0:T(8,128)}, u32[]{:S(2)}, u32[]{:S(2)}) %all-to-all-start.1) | async-done | bytes 4194336 | tf_op jit(solution)/shard_map/all_to_all | solution.py:144
  321.8 6.2 %fusion.40 = f32[16,4096,1]{1,0,2:T(8,128)S(1)} fusion(f32[16,16,16]{1,2,0:T(8,128)S(1)} %fusion.7, f32[16,16,4096]{2,1,0:T(8,128)} %all-to-all-done.1), kind=kOutput, calls=%fused_computation.75 | convolution fusion | flops 201326592 | bytes 4472832 | tf_op jit(solution)/shard_map/pqb,pqf->bf/dot_general | solution.py:145
  328.2 0.7 broadcast_multiply_fusion
  (26 shorter events, 0.6 us)
Async XLA Ops:
  6.5 44.6 %all-gather.2.cloned.1.call-start = ((), (), s32[]{:S(2)}) async-start(), calls=%async_computation.2 | async-start | bytes 2228224 | tf_op jit(solution)/shard_map/all_gather | solution.py:89
  10.0 144.1 %all-reduce.3.cloned.1.call-start = ((), (), s32[]{:S(2)}) async-start(), calls=%async_computation.3 | async-start | bytes 2097152
  60.5 2.0 copy-start.1
  60.5 2.0 copy-start.2
  60.5 2.3 copy-start.4
  60.5 3.6 %copy-start.3 = (s32[2048]{0:T(1024)S(1)}, s32[2048]{0:T(1024)}, u32[]{:S(2)}) copy-start(s32[2048]{0:T(1024)} %param.22) | copy-start | bytes 24580
  157.1 54.2 %all-to-all-start = ((bf16[16,16,4096]{2,1,0:T(8,128)(2,1)}), bf16[16,16,4096]{2,1,0:T(8,128)(2,1)S(1)}, u32[]{:S(2)}, u32[]{:S(2)}) async-start(bf16[16,16,4096]{2,1,0:T(8,128)(2,1)} %convolution_convert_fusion), calls=%async_computation | async-start | bytes 4194304 | tf_op jit(solution)/shard_map/all_to_all | solution.py:127
  224.3 5.3 %copy-start = (s32[2048]{0:T(1024)S(1)}, s32[2048]{0:T(1024)}, u32[]{:S(2)}) copy-start(s32[2048]{0:T(1024)} %param.20) | copy-start | bytes 24580
  224.3 97.5 %all-to-all-start.1 = ((f32[16,16,4096]{2,1,0:T(8,128)}), f32[16,16,4096]{2,1,0:T(8,128)}, u32[]{:S(2)}, u32[]{:S(2)}) async-start(f32[16,16,4096]{2,1,0:T(8,128)} %fusion.11), calls=%async_computation.1 | async-start | bytes 8388608 | tf_op jit(solution)/shard_map/all_to_all | solution.py:144
Sparse Core Ops, SparseCore 0:
  10.1 41.0 all-gather.1
  62.6 91.4 all-reduce.2
where the time goes:
time: 336 us
  waiting for transfers between devices  268 us (80%)
  matrix products  29.6 us (9%)
  between operations  14.3 us (4%)
  starting transfers between devices  11.8 us (4%)
  local copies, waits for them, and re-layouts  6.41 us (2%)
  other arithmetic  5.89 us (2%)
    all_to_all x1, waiting for transfers between devices, shards(): lax.all_to_all(returned, 'tile', split_axis=0, concat_axis=0, tiled=True)  92 us
    unnamed x3, waiting for transfers between devices  89.8 us
    all_to_all x1, waiting for transfers between devices, shards(): lax.all_to_all(outgoing_data, 'tile', split_axis=0, concat_axis=0, tiled=...  47 us
    all_gather x1, waiting for transfers between devices, shards(): piece = lax.all_gather(cell_rows, 'tile', axis=0, tiled=True)  38.9 us
    all_to_all x1, starting transfers between devices, shards(): lax.all_to_all(outgoing_data, 'tile', split_axis=0, concat_axis=0, tiled=...  6.76 us
  transfers between devices with their start and end apart: 4, of which 4 were waited for; matrix products, arithmetic and copies ran while one was open for 1% of the time, Pallas kernels for 0%

commit v1 on v0

--- a/solution.py
+++ b/solution.py
@@ -86,7 +86,26 @@
     col_global = col_owner_mine * cell_blocks + col_local_mine
     col_slots = receiver_table(col_owner_mine, capacity, peer_count)
     col_choice = sender_table(col_owner_all, col_local_all, own_index, capacity, cell_blocks)
-    piece = lax.all_gather(cell_rows, "tile", axis=0, tiled=True)
+    size, index, rows = (lax.axis_size("tile"), lax.axis_index("tile"), cell_rows.shape[0])
+    upward = [(i, (i + 1) % size) for i in range(size)]
+    left = [(i, (i - 1) % size) for i in range(size)]
+    filled = jnp.zeros(
+        (*cell_rows.shape[:0], size * rows, *cell_rows.shape[0 + 1 :]), cell_rows.dtype
+    )
+    filled = lax.dynamic_update_slice_in_dim(filled, cell_rows, index * rows, axis=0)
+    from_left = from_right = cell_rows
+    halfway = size // 2
+    for step in range(1, halfway + 1):
+        from_left = lax.ppermute(from_left, "tile", upward)
+        filled = lax.dynamic_update_slice_in_dim(
+            filled, from_left, (index - step) % size * rows, axis=0
+        )
+        if step < size - halfway:
+            from_right = lax.ppermute(from_right, "tile", left)
+            filled = lax.dynamic_update_slice_in_dim(
+                filled, from_right, (index + step) % size * rows, axis=0
+            )
+    piece = filled
     rows_here = piece.shape[0]
     match = (col_global[:, None] == jnp.arange(rows_here, dtype=jnp.int32)[None, :]).astype(
         jnp.bfloat16

time: 336 us -> 347 us (1.033)
  starting transfers between devices: 11.8 us -> 37.5 us
  waiting for transfers between devices: 268 us -> 255 us
    all_gather x1 -> x0, waiting for transfers between devices: 38.9 us -> none  [shards(): piece = lax.all_gather(cell_rows, 'tile', axis=0, tiled=True)]
    ppermute x0 -> x15, starting transfers between devices: none -> 25.8 us  [the longest x8 25.8 us: shards(): from_left = lax.ppermute(from_left, 'tile', upward)]
    ppermute x0 -> x15, waiting for transfers between devices: none -> 13.3 us  [the longest x8 13.3 us: shards(): from_left = lax.ppermute(from_left, 'tile', upward)]
    unnamed x3 -> x2, waiting for transfers between devices: 89.8 us -> 103 us
  transfers between devices with their start and end apart: 4 -> 18, of which waited for: 4 -> 10; matrix products, arithmetic and copies ran while one was open for 1% -> 1% of each run, Pallas kernels for 0% -> 0%
where the time goes in v1:
time: 347 us; the launch traced here: 346 us
  waiting for transfers between devices  255 us (73%)
  starting transfers between devices  37.5 us (11%)
  matrix products  28 us (8%)
  between operations  14.6 us (4%)
  local copies, waits for them, and re-layouts  6.21 us (2%)
  other arithmetic  5.18 us (1%)
    unnamed x2, waiting for transfers between devices  103 us
    all_to_all x1, waiting for transfers between devices, shards(): lax.all_to_all(returned, 'tile', split_axis=0, concat_axis=0, tiled=True)  92 us
    all_to_all x1, waiting for transfers between devices, shards(): lax.all_to_all(outgoing_data, 'tile', split_axis=0, concat_axis=0, tiled=...  47 us
    ppermute x8, starting transfers between devices, shards(): from_left = lax.ppermute(from_left, 'tile', upward)  25.8 us
    ppermute x8, waiting for transfers between devices, shards(): from_left = lax.ppermute(from_left, 'tile', upward)  13.3 us
  transfers between devices with their start and end apart: 18, of which 10 were waited for; matrix products, arithmetic and copies ran while one was open for 1% of the time, Pallas kernels for 0%

profile of v1, /device:TPU:13, one launch (start us, length us, event | category | flops | bytes accessed | tf_op | source)
XLA Modules:
  0.0 346.4 jit_solution(1906103821012045004)
XLA Ops:
  6.6 0.9 select_reduce_fusion
  7.5 0.8 add_divide_fusion
  8.3 1.0 multiply_convert_fusion
  9.3 1.9 collective-permute-start
  13.3 3.2 collective-permute-start.2
  16.6 1.9 collective-permute-done.2
  18.5 3.4 collective-permute-start.4
  22.0 1.9 collective-permute-done.4
  23.9 3.4 collective-permute-start.6
  27.4 1.9 collective-permute-done.6
  29.3 3.4 collective-permute-start.8
  32.8 1.9 collective-permute-done.8
  34.7 3.4 collective-permute-start.10
  38.2 1.9 collective-permute-done.10
  40.1 3.4 collective-permute-start.12
  43.6 1.9 collective-permute-done.12
  45.5 3.4 collective-permute-start.14
  49.0 1.9 collective-permute-done.14
  51.8 5.2 %fusion.3 = f32[128,8,512]{2,1,0:T(8,128)S(1)} fusion(bf16[128,32,512]{2,1,0:T(8,128)(2,1)} %param.17, bf16[128,8,512]{2,1,0:T(8,128)(2,1)S(1)} %bitcast.63, bf16[128,32,512]{2,1,0:T(8,128)(2,1)} %param.18, f32[128,32]{1,0:T(8,128)S(1)} %fusion.23), kind=kOutput, calls=%fused_computation.8 | convolution fusion | flops 67174400 | bytes 11550720 | tf_op jit(solution)/shard_map/tkr,trs->tks/dot_general | solution.py:120
  57.0 1.6 copy.17
  58.6 1.9 fusion.28
  62.3 102.6 %all-reduce.3.cloned.1.call-done = f32[64,4096]{1,0:T(8,128)} async-done(((f32[64,4096]{1,0:T(8,128)}), f32[64,4096]{1,0:T(8,128)}) %all-reduce.3.cloned.1.call-update) | async-done | bytes 1048592
  164.9 3.1 convolution_convert_fusion
  167.9 6.8 %all-to-all-start = ((bf16[16,16,4096]{2,1,0:T(8,128)(2,1)}), bf16[16,16,4096]{2,1,0:T(8,128)(2,1)S(1)}, u32[]{:S(2)}, u32[]{:S(2)}) async-start(bf16[16,16,4096]{2,1,0:T(8,128)(2,1)} %convolution_convert_fusion), calls=%async_computation | async-start | bytes 4194304 | tf_op jit(solution)/shard_map/all_to_all | solution.py:146
  175.1 47.0 %all-to-all-done = bf16[16,16,4096]{2,1,0:T(8,128)(2,1)S(1)} async-done(((bf16[16,16,4096]{2,1,0:T(8,128)(2,1)}), bf16[16,16,4096]{2,1,0:T(8,128)(2,1)S(1)}, u32[]{:S(2)}, u32[]{:S(2)}) %all-to-all-start) | async-done | bytes 2097184 | tf_op jit(solution)/shard_map/all_to_all | solution.py:146
  223.0 6.5 %fusion.2 = f32[128,8,512]{2,1,0:T(8,128)} fusion(bf16[128,32,512]{2,1,0:T(8,128)(2,1)} %param.18, bf16[128,8,512]{2,1,0:T(8,128)(2,1)S(1)} %bitcast.62, bf16[128,32,512]{2,1,0:T(8,128)(2,1)} %param.17, f32[128,32]{1,0:T(8,128)S(1)} %fusion.23), kind=kOutput, calls=%fused_computation.7 | convolution fusion | flops 67174400 | bytes 11550720 | tf_op jit(solution)/shard_map/tkr,trc->tkc/dot_general | solution.py:156
  229.6 1.7 reshape.169
  231.3 3.8 %fusion.11 = f32[16,16,4096]{2,1,0:T(8,128)} fusion(f32[128,4096,1]{1,0,2:T(8,128)S(1)} %reshape.169, s32[16,16]{1,0:T(8,128)S(1)} %multiply_add_fusion, s32[128]{0:T(128)S(1)} %multiply_add_fusion.2), kind=kOutput, calls=%fused_computation.25 | convolution fusion | flops 1610645504 | bytes 6292992 | tf_op jit(solution)/shard_map/pqt,tf->pqf/dot_general | solution.py:160
  235.1 4.9 %all-to-all-start.1 = ((f32[16,16,4096]{2,1,0:T(8,128)}), f32[16,16,4096]{2,1,0:T(8,128)}, u32[]{:S(2)}, u32[]{:S(2)}) async-start(f32[16,16,4096]{2,1,0:T(8,128)} %fusion.11), calls=%async_computation.1 | async-start | bytes 8388608 | tf_op jit(solution)/shard_map/all_to_all | solution.py:163
  240.5 92.0 %all-to-all-done.1 = f32[16,16,4096]{2,1,0:T(8,128)} async-done(((f32[16,16,4096]{2,1,0:T(8,128)}), f32[16,16,4096]{2,1,0:T(8,128)}, u32[]{:S(2)}, u32[]{:S(2)}) %all-to-all-start.1) | async-done | bytes 4194336 | tf_op jit(solution)/shard_map/all_to_all | solution.py:163
  332.5 6.2 %fusion.40 = f32[16,4096,1]{1,0,2:T(8,128)S(1)} fusion(f32[16,16,16]{1,2,0:T(8,128)S(1)} %fusion.7, f32[16,16,4096]{2,1,0:T(8,128)} %all-to-all-done.1), kind=kOutput, calls=%fused_computation.91 | convolution fusion | flops 201326592 | bytes 4472832 | tf_op jit(solution)/shard_map/pqb,pqf->bf/dot_general | solution.py:164
  338.8 0.7 broadcast_multiply_fusion
  (70 shorter events, 5.9 us)
Async XLA Ops:
  6.5 5.6 %copy-start.1 = (s32[2048,1]{0,1:T(1,128)S(1)}, s32[2048,1]{0,1:T(1,128)}, u32[]{:S(2)}) copy-start(s32[2048,1]{0,1:T(1,128)} %param.21) | copy-start | bytes 24580
  6.5 5.6 %copy-start.3 = (s32[2048]{0:T(1024)S(1)}, s32[2048]{0:T(1024)}, u32[]{:S(2)}) copy-start(s32[2048]{0:T(1024)} %param.22) | copy-start | bytes 24580
  6.5 6.7 %copy-start.2 = (s32[2048,1]{0,1:T(1,128)S(1)}, s32[2048,1]{0,1:T(1,128)}, u32[]{:S(2)}) copy-start(s32[2048,1]{0,1:T(1,128)} %param.19) | copy-start | bytes 24580
  6.5 6.7 %copy-start = (s32[2048]{0:T(1024)S(1)}, s32[2048]{0:T(1024)}, u32[]{:S(2)}) copy-start(s32[2048]{0:T(1024)} %param.20) | copy-start | bytes 24580
  6.5 158.3 %all-reduce.3.cloned.1.call-start = ((), (), s32[]{:S(2)}) async-start(), calls=%async_computation.2 | async-start | bytes 2097152
  9.3 4.0 %collective-permute-start = (bf16[16,4096]{1,0:T(8,128)(2,1)S(1)}, bf16[16,4096]{1,0:T(8,128)(2,1)S(1)}, u32[]{:S(2)}, u32[]{:S(2)}) collective-permute-start(bf16[16,4096]{1,0:T(8,128)(2,1)S(1)} %bitcast.66), channel_id=1, source_target_pairs={{0,1},{1,2},{2,3},{3,4},{4,5},{5,6},{6,7},{7,8},{8,9},{9,10},{10,1... | collective-permute-start | bytes 393224 | tf_op jit(solution)/shard_map/ppermute | solution.py:99
  11.2 5.3 %collective-permute-start.1 = (bf16[16,4096]{1,0:T(8,128)(2,1)S(1)}, bf16[16,4096]{1,0:T(8,128)(2,1)S(1)}, u32[]{:S(2)}, u32[]{:S(2)}) collective-permute-start(bf16[16,4096]{1,0:T(8,128)(2,1)S(1)} %bitcast.67), channel_id=1, source_target_pairs={{0,15},{1,0},{2,1},{3,2},{4,3},{5,4},{6,5},{7,6},{8,7},{9,8},{10,9... | collective-permute-start | bytes 393224 | tf_op jit(solution)/shard_map/ppermute | solution.py:104
  13.3 5.2 %collective-permute-start.2 = (bf16[16,4096]{1,0:T(8,128)(2,1)S(1)}, bf16[16,4096]{1,0:T(8,128)(2,1)S(1)}, u32[]{:S(2)}, u32[]{:S(2)}) collective-permute-start(bf16[16,4096]{1,0:T(8,128)(2,1)S(1)} %collective-permute-done), channel_id=1, source_target_pairs={{0,1},{1,2},{2,3},{3,4},{4,5},{5,6},{6,7},{7,8},{8,9},{9,10},{10,1... | collective-permute-start | bytes 393224 | tf_op jit(solution)/shard_map/ppermute | solution.py:99
  16.5 5.4 %collective-permute-start.3 = (bf16[16,4096]{1,0:T(8,128)(2,1)S(1)}, bf16[16,4096]{1,0:T(8,128)(2,1)S(1)}, u32[]{:S(2)}, u32[]{:S(2)}) collective-permute-start(bf16[16,4096]{1,0:T(8,128)(2,1)S(1)} %collective-permute-done.1), channel_id=1, source_target_pairs={{0,15},{1,0},{2,1},{3,2},{4,3},{5,4},{6,5},{7,6},{8,7},{9,8},{10,9... | collective-permute-start | bytes 393224 | tf_op jit(solution)/shard_map/ppermute | solution.py:104
  18.5 5.4 %collective-permute-start.4 = (bf16[16,4096]{1,0:T(8,128)(2,1)S(1)}, bf16[16,4096]{1,0:T(8,128)(2,1)S(1)}, u32[]{:S(2)}, u32[]{:S(2)}) collective-permute-start(bf16[16,4096]{1,0:T(8,128)(2,1)S(1)} %collective-permute-done.2), channel_id=1, source_target_pairs={{0,1},{1,2},{2,3},{3,4},{4,5},{5,6},{6,7},{7,8},{8,9},{9,10},{10,1... | collective-permute-start | bytes 393224 | tf_op jit(solution)/shard_map/ppermute | solution.py:99
  21.9 5.4 %collective-permute-start.5 = (bf16[16,4096]{1,0:T(8,128)(2,1)S(1)}, bf16[16,4096]{1,0:T(8,128)(2,1)S(1)}, u32[]{:S(2)}, u32[]{:S(2)}) collective-permute-start(bf16[16,4096]{1,0:T(8,128)(2,1)S(1)} %collective-permute-done.3), channel_id=1, source_target_pairs={{0,15},{1,0},{2,1},{3,2},{4,3},{5,4},{6,5},{7,6},{8,7},{9,8},{10,9... | collective-permute-start | bytes 393224 | tf_op jit(solution)/shard_map/ppermute | solution.py:104
  23.9 5.4 %collective-permute-start.6 = (bf16[16,4096]{1,0:T(8,128)(2,1)S(1)}, bf16[16,4096]{1,0:T(8,128)(2,1)S(1)}, u32[]{:S(2)}, u32[]{:S(2)}) collective-permute-start(bf16[16,4096]{1,0:T(8,128)(2,1)S(1)} %collective-permute-done.4), channel_id=1, source_target_pairs={{0,1},{1,2},{2,3},{3,4},{4,5},{5,6},{6,7},{7,8},{8,9},{9,10},{10,1... | collective-permute-start | bytes 393224 | tf_op jit(solution)/shard_map/ppermute | solution.py:99
  27.3 5.4 %collective-permute-start.7 = (bf16[16,4096]{1,0:T(8,128)(2,1)S(1)}, bf16[16,4096]{1,0:T(8,128)(2,1)S(1)}, u32[]{:S(2)}, u32[]{:S(2)}) collective-permute-start(bf16[16,4096]{1,0:T(8,128)(2,1)S(1)} %collective-permute-done.5), channel_id=1, source_target_pairs={{0,15},{1,0},{2,1},{3,2},{4,3},{5,4},{6,5},{7,6},{8,7},{9,8},{10,9... | collective-permute-start | bytes 393224 | tf_op jit(solution)/shard_map/ppermute | solution.py:104
  29.3 5.4 %collective-permute-start.8 = (bf16[16,4096]{1,0:T(8,128)(2,1)S(1)}, bf16[16,4096]{1,0:T(8,128)(2,1)S(1)}, u32[]{:S(2)}, u32[]{:S(2)}) collective-permute-start(bf16[16,4096]{1,0:T(8,128)(2,1)S(1)} %collective-permute-done.6), channel_id=1, source_target_pairs={{0,1},{1,2},{2,3},{3,4},{4,5},{5,6},{6,7},{7,8},{8,9},{9,10},{10,1... | collective-permute-start | bytes 393224 | tf_op jit(solution)/shard_map/ppermute | solution.py:99
  32.7 5.4 %collective-permute-start.9 = (bf16[16,4096]{1,0:T(8,128)(2,1)S(1)}, bf16[16,4096]{1,0:T(8,128)(2,1)S(1)}, u32[]{:S(2)}, u32[]{:S(2)}) collective-permute-start(bf16[16,4096]{1,0:T(8,128)(2,1)S(1)} %collective-permute-done.7), channel_id=1, source_target_pairs={{0,15},{1,0},{2,1},{3,2},{4,3},{5,4},{6,5},{7,6},{8,7},{9,8},{10,9... | collective-permute-start | bytes 393224 | tf_op jit(solution)/shard_map/ppermute | solution.py:104
  34.7 5.4 %collective-permute-start.10 = (bf16[16,4096]{1,0:T(8,128)(2,1)S(1)}, bf16[16,4096]{1,0:T(8,128)(2,1)S(1)}, u32[]{:S(2)}, u32[]{:S(2)}) collective-permute-start(bf16[16,4096]{1,0:T(8,128)(2,1)S(1)} %collective-permute-done.8), channel_id=1, source_target_pairs={{0,1},{1,2},{2,3},{3,4},{4,5},{5,6},{6,7},{7,8},{8,9},{9,10},{10,1... | collective-permute-start | bytes 393224 | tf_op jit(solution)/shard_map/ppermute | solution.py:99
  38.1 5.4 %collective-permute-start.11 = (bf16[16,4096]{1,0:T(8,128)(2,1)S(1)}, bf16[16,4096]{1,0:T(8,128)(2,1)S(1)}, u32[]{:S(2)}, u32[]{:S(2)}) collective-permute-start(bf16[16,4096]{1,0:T(8,128)(2,1)S(1)} %collective-permute-done.9), channel_id=1, source_target_pairs={{0,15},{1,0},{2,1},{3,2},{4,3},{5,4},{6,5},{7,6},{8,7},{9,8},{10,9... | collective-permute-start | bytes 393224 | tf_op jit(solution)/shard_map/ppermute | solution.py:104
  40.1 5.4 %collective-permute-start.12 = (bf16[16,4096]{1,0:T(8,128)(2,1)S(1)}, bf16[16,4096]{1,0:T(8,128)(2,1)S(1)}, u32[]{:S(2)}, u32[]{:S(2)}) collective-permute-start(bf16[16,4096]{1,0:T(8,128)(2,1)S(1)} %collective-permute-done.10), channel_id=1, source_target_pairs={{0,1},{1,2},{2,3},{3,4},{4,5},{5,6},{6,7},{7,8},{8,9},{9,10},{10,1... | collective-permute-start | bytes 393224 | tf_op jit(solution)/shard_map/ppermute | solution.py:99
  43.5 5.4 %collective-permute-start.13 = (bf16[16,4096]{1,0:T(8,128)(2,1)S(1)}, bf16[16,4096]{1,0:T(8,128)(2,1)S(1)}, u32[]{:S(2)}, u32[]{:S(2)}) collective-permute-start(bf16[16,4096]{1,0:T(8,128)(2,1)S(1)} %collective-permute-done.11), channel_id=1, source_target_pairs={{0,15},{1,0},{2,1},{3,2},{4,3},{5,4},{6,5},{7,6},{8,7},{9,8},{10,9... | collective-permute-start | bytes 393224 | tf_op jit(solution)/shard_map/ppermute | solution.py:104
  45.5 5.4 %collective-permute-start.14 = (bf16[16,4096]{1,0:T(8,128)(2,1)S(1)}, bf16[16,4096]{1,0:T(8,128)(2,1)S(1)}, u32[]{:S(2)}, u32[]{:S(2)}) collective-permute-start(bf16[16,4096]{1,0:T(8,128)(2,1)S(1)} %collective-permute-done.12), channel_id=1, source_target_pairs={{0,1},{1,2},{2,3},{3,4},{4,5},{5,6},{6,7},{7,8},{8,9},{9,10},{10,1... | collective-permute-start | bytes 393224 | tf_op jit(solution)/shard_map/ppermute | solution.py:99
  58.6 2.3 copy-start.4
  167.9 54.2 %all-to-all-start = ((bf16[16,16,4096]{2,1,0:T(8,128)(2,1)}), bf16[16,16,4096]{2,1,0:T(8,128)(2,1)S(1)}, u32[]{:S(2)}, u32[]{:S(2)}) async-start(bf16[16,16,4096]{2,1,0:T(8,128)(2,1)} %convolution_convert_fusion), calls=%async_computation | async-start | bytes 4194304 | tf_op jit(solution)/shard_map/all_to_all | solution.py:146
  235.1 97.4 %all-to-all-start.1 = ((f32[16,16,4096]{2,1,0:T(8,128)}), f32[16,16,4096]{2,1,0:T(8,128)}, u32[]{:S(2)}, u32[]{:S(2)}) async-start(f32[16,16,4096]{2,1,0:T(8,128)} %fusion.11), calls=%async_computation.1 | async-start | bytes 8388608 | tf_op jit(solution)/shard_map/all_to_all | solution.py:163
Sparse Core Ops, SparseCore 0:
  60.6 104.1 all-reduce.2
